TPU v7x, 256 devices: a whole 4x4x8 slice. The times are simulated.
256 devices in a mesh: region: 8 (over y, core), sub: 32 (over x, z).
Axes of the slice: x: 4, y: 4, z: 8, core: 2. Of those that a mesh axis runs over, the one named last changes fastest.
Arguments:
- probes: bfloat16 [32, 3407872], P(None, ('region', 'sub')), may hold values from -6 to 6
- blocks: bfloat16 [26624, 3, 128, 128], P(('region', 'sub')), may hold values from -0.109375 to 0.109375
- col_slot: int32 [26624, 3], P(('region', 'sub')), may hold values from 0 to 127, as said below
- send_sub: int32 [256, 2, 8], P(('region', 'sub')), may hold values from -1 to 103, as said below
- send_reg: int32 [256, 2, 4], P(('region', 'sub')), may hold values from -1 to 103, as said below
- coeffs: float32 [9], replicated, may hold values from 0.3 to 1
Outputs:
- filtered: float32 [32, 3407872], P(None, ('region', 'sub'))
Inputs may be any that keep to these rules, and one draw needn't show every extreme that they name: `col_slot`: entry 0 of each block row names the row's own block. Slots from 104 on name received blocks in this order: 8 from the lower sub neighbour, 8 from the upper sub neighbour, 4 from the lower region neighbour, 4 from the upper one; only received slots that the sender fills are named, and each of those is named by some row. send_sub[d, 0] lists rows sent to sub index one lower in the same region, send_sub[d, 1] to one higher: distinct rows first, then -1; devices at the ends of the sub axis send nothing outward; some list is full. send_reg[d, 0] lists rows sent to the same sub index in the region one lower, send_reg[d, 1] one higher: distinct rows first, then -1; the first and last regions send nothing outward; some list is full.
All inputs are finite; a program needn't handle non-finite values.
Results may differ from a plain program's by a relative error of at most 0.0065.
Values may be sent and summed in bfloat16 or wider, within the bound.
A program may use at most 128 MiB of HBM per device.

v0:
```python
import jax
import jax.numpy as jnp
from jax import lax
from jax.experimental import pallas as pl
from jax.experimental.pallas import tpu as pltpu
from jax.sharding import PartitionSpec as P

BLK = 128
NNZ = 3
PROBES = 32
DEG = 8
ROWS = 104
HS = 8
HR = 4
HALO = 2 * HS + 2 * HR
UNIT = 8
UNITS = ROWS // UNIT
F32 = jnp.float32
BF16 = jnp.bfloat16
MESH = pl.DeviceIdType.MESH
cat = jnp.concatenate


def kernel(probes_hbm, blocks_hbm, col, send_sub, send_reg, coeffs, out_hbm,
           probes, raw, weights, state, landing, outgoing, cheb, total,
           in_sem, out_sem, send_sem, recv_sem):
    region = lax.axis_index("region")
    sub = lax.axis_index("sub")
    n_region = lax.axis_size("region")
    n_sub = lax.axis_size("sub")
    links = (
        (0, HS, "sub", lax.rem(sub + 1, n_sub)),
        (HS, HS, "sub", lax.rem(sub + n_sub - 1, n_sub)),
        (2 * HS, HR, "region", lax.rem(region + 1, n_region)),
        (2 * HS + HR, HR, "region", lax.rem(region + n_region - 1, n_region)),
    )

    def load_rows(u):
        rows = pl.ds(u * UNIT, UNIT)
        return pltpu.make_async_copy(blocks_hbm.at[rows], raw.at[rows], in_sem.at[u])

    probes_copy = pltpu.make_async_copy(probes_hbm, probes, in_sem.at[UNITS])
    probes_copy.start()
    for u in range(UNITS):
        load_rows(u).start()
    barrier = pltpu.get_barrier_semaphore()
    for _, _, axis, target in links:
        pl.semaphore_signal(barrier, inc=1, device_id={axis: target}, device_id_type=MESH)

    def listed(slot):
        if slot < HS:
            row = send_sub[0, 1, slot]
        elif slot < 2 * HS:
            row = send_sub[0, 0, slot - HS]
        elif slot < 2 * HS + HR:
            row = send_reg[0, 1, slot - 2 * HS]
        else:
            row = send_reg[0, 0, slot - 2 * HS - HR]
        return jnp.maximum(row, 0)

    def halo_copy(step, link):
        first, count, axis, target = links[link]
        slots = pl.ds(first, count)
        return pltpu.make_async_remote_copy(
            src_ref=outgoing.at[step, slots],
            dst_ref=landing.at[step, slots],
            send_sem=send_sem.at[step, link],
            recv_sem=recv_sem.at[step, link],
            device_id={axis: target},
            device_id_type=MESH,
        )

    def take_halo(step):
        for link in range(4):
            halo_copy(step, link).wait_recv()
        now = lax.rem(step, 2)
        for slot in range(HALO):
            state[now, ROWS + slot] = landing[step, slot]

    probes_copy.wait()
    first_coeff = coeffs[0]
    for i in range(ROWS):
        block = probes[:, i * BLK:(i + 1) * BLK]
        state[0, i] = block
        wide = block.astype(F32)
        cheb[0, i] = wide
        cheb[1, i] = jnp.zeros_like(wide)
        total[:, i * BLK:(i + 1) * BLK] = first_coeff * wide
    for slot in range(HALO):
        outgoing[0, slot] = state[0, listed(slot)]
    pl.semaphore_wait(barrier, 4)
    for link in range(4):
        halo_copy(0, link).start()

    def transpose_unit(u, carry):
        load_rows(u).wait()
        for i in range(UNIT):
            for k in range(NNZ):
                weights[u * UNIT + i, k] = raw[u * UNIT + i, k].T
        return carry

    lax.fori_loop(0, UNITS, transpose_unit, 0)
    take_halo(0)

    zero = jnp.zeros((PROBES, BLK), BF16)

    def issue(now, rows, accs):
        taken = [[state[now, col[r, k]] for k in range(NNZ)] for r in rows]
        for tile in range(3):
            for m in range(2):
                r = rows[4 * m:4 * m + 4]
                v = taken[4 * m:4 * m + 4]
                if tile < 2:
                    a, b = 2 * tile, 2 * tile + 1
                    rhs = cat([cat([weights[r[a], k], weights[r[b], k]], 1) for k in range(2)], 0)
                else:
                    rhs = cat([cat([weights[r[a], 2], weights[r[a + 1], 2]], 1) for a in (0, 2)], 0)
                staged = tile % 2
                pltpu.matmul_push_rhs(rhs, staged, m)
                if tile < 2:
                    lhs = cat([cat([v[a][0], v[a][1]], 1), cat([v[b][0], v[b][1]], 1)], 0)
                    pltpu.matmul_acc_lhs(accs[m][tile], lhs, staged)
                else:
                    upper = cat([cat([v[0][2], zero], 1), cat([v[1][2], zero], 1)], 0)
                    lower = cat([cat([zero, v[2][2]], 1), cat([zero, v[3][2]], 1)], 0)
                    pltpu.matmul_acc_lhs(accs[m][0], upper, staged)
                    pltpu.matmul_acc_lhs(accs[m][1], lower)

    def products(accs):
        result = []
        for m in range(2):
            for half in range(2):
                both = pltpu.matmul_pop(accs[m][half])
                result.append(both[:PROBES, :BLK])
                result.append(both[PROBES:, BLK:])
        return result

    def run(*a):
        sets = (((a[0], a[1]), (a[2], a[3])), ((a[4], a[5]), (a[6], a[7])))

        def one_step(step, carry):
            now = lax.rem(step, 2)
            later = 1 - now
            scale = jnp.where(step == 0, 1.0, 2.0).astype(F32)
            coeff = coeffs[step + 1]

            def finish_listed(unit, accs):
                for i, product in enumerate(products(accs)):
                    slot = unit * UNIT + i
                    new = scale * product - cheb[later, listed(slot)]
                    outgoing[step + 1, slot] = new.astype(BF16)

            def finish(unit, accs):
                for i, product in enumerate(products(accs)):
                    row = unit * UNIT + i
                    columns = slice(row * BLK, (row + 1) * BLK)
                    new = scale * product - cheb[later, row]
                    cheb[later, row] = new
                    state[later, row] = new.astype(BF16)
                    total[:, columns] += coeff * new

            @pl.when(step < DEG - 1)
            def _():
                for unit in range(3):
                    issue(now, [listed(unit * UNIT + i) for i in range(UNIT)], sets[unit % 2])
                    if unit == 1:
                        finish_listed(0, sets[0])
                        halo_copy(step + 1, 0).start()
                    elif unit == 2:
                        finish_listed(1, sets[1])
                        halo_copy(step + 1, 1).start()
                finish_listed(2, sets[0])
                halo_copy(step + 1, 2).start()
                halo_copy(step + 1, 3).start()

            for unit in range(UNITS):
                issue(now, [unit * UNIT + i for i in range(UNIT)], sets[unit % 2])
                if unit:
                    finish(unit - 1, sets[(unit - 1) % 2])
            finish(UNITS - 1, sets[(UNITS - 1) % 2])

            @pl.when(step < DEG - 1)
            def _():
                take_halo(step + 1)

            return carry

        lax.fori_loop(0, DEG, one_step, 0)

    pl.run_scoped(run, *[pltpu.ACC(mxu_id=m)((2 * PROBES, 2 * BLK), F32) for m in (0, 0, 1, 1, 0, 0, 1, 1)])

    out_copy = pltpu.make_async_copy(total, out_hbm, out_sem)
    out_copy.start()

    def sent(step, carry):
        for link in range(4):
            halo_copy(step, link).wait_send()
        return carry

    lax.fori_loop(0, DEG, sent, 0)
    out_copy.wait()


def local(probes, blocks, col_slot, send_sub, send_reg, coeffs):
    anywhere = pl.BlockSpec(memory_space=pl.ANY)
    scalar = pl.BlockSpec(memory_space=pltpu.SMEM)
    width = ROWS * BLK
    return pl.pallas_call(
        kernel,
        out_shape=jax.ShapeDtypeStruct((PROBES, width), F32),
        in_specs=[anywhere, anywhere, scalar, scalar, scalar, scalar],
        out_specs=anywhere,
        scratch_shapes=[
            pltpu.VMEM((PROBES, width), BF16),
            pltpu.VMEM((ROWS, NNZ, BLK, BLK), BF16),
            pltpu.VMEM((ROWS, NNZ, BLK, BLK), BF16),
            pltpu.VMEM((2, ROWS + HALO, PROBES, BLK), BF16),
            pltpu.VMEM((DEG, HALO, PROBES, BLK), BF16),
            pltpu.VMEM((DEG, HALO, PROBES, BLK), BF16),
            pltpu.VMEM((2, ROWS, PROBES, BLK), F32),
            pltpu.VMEM((PROBES, width), F32),
            pltpu.SemaphoreType.DMA((UNITS + 1,)),
            pltpu.SemaphoreType.DMA,
            pltpu.SemaphoreType.DMA((DEG, 4)),
            pltpu.SemaphoreType.DMA((DEG, 4)),
        ],
        compiler_params=pltpu.CompilerParams(
            collective_id=0, has_side_effects=True, vmem_limit_bytes=56 << 20
        ),
    )(probes, blocks, col_slot, send_sub, send_reg, coeffs)


def solution(mesh):
    both = ("region", "sub")
    mapped = jax.shard_map(
        local,
        mesh=mesh,
        in_specs=(
            P(None, both),
            P(both, None, None, None),
            P(both, None),
            P(both, None, None),
            P(both, None, None),
            P(),
        ),
        out_specs=P(None, both),
        check_vma=False,
    )

    def run(*args):
        with jax.sharding.use_abstract_mesh(mesh.abstract_mesh):
            return mapped(*args)

    return run
```

profile of v0, /device:TPU:8, one launch (start us, length us, event | category | flops | bytes accessed | tf_op | source)
XLA Modules:
  0.0 59.9 jit_solution(16234686983054798692)
XLA Ops:
  0.0 1.4 %copy.7.col = s32[104,3]{1,0:T(8,128)} copy(s32[104,3]{0,1:T(4,128)} %param.8) | data formatting | bytes 2496 | tf_op args[2]
  1.4 55.7 %shard_map.64 = f32[32,13312]{1,0:T(8,128)} custom-call(bf16[32,13312]{1,0:T(8,128)(2,1)} %probes_hbm.1, bf16[104,3,128,128]{3,2,1,0:T(8,128)(2,1)} %blocks_hbm.1, s32[104,3]{1,0:T(8,128)} %copy.7.col, s32[1,2,8]{2,1,0:T(2,128)} %send_sub.1, s32[1,2,4]{2,1,0:T(2,128)} %send_reg.1, f32[9]{0:T(128)} %coeffs.1), custom_call_target="tpu_custom_call" | custom-call | tf_op jit(solution)/shard_map/pallas_call | solution.py:208
  57.1 2.7 %copy.9 = f32[32,13312]{1,0:T(8,128)} copy(f32[32,13312]{1,0:T(8,128)} %shard_map.64) | data formatting | bytes 3407872
where the time goes:
time: 60.1 us; the launch traced here: 59.9 us
  Pallas kernels  55.7 us (93%)
  local copies, waits for them, and re-layouts  4.15 us (7%)
    pallas_call x1, Pallas kernels, local(): pl.pallas_call(kernel, out_shape=jax.ShapeDtypeStruct((PROBES, width), F3...  55.7 us
    unnamed x2, local copies, waits for them, and re-layouts  4.15 us

commit v1 on v0

v1 whole, which is shorter than its diff:
```python
import jax
import jax.numpy as jnp
from jax import lax
from jax.experimental import pallas as pl
from jax.experimental.pallas import tpu as pltpu
from jax.sharding import PartitionSpec as P

BLK = 128
NNZ = 3
PROBES = 32
DEG = 8
ROWS = 104
HS = 8
HR = 4
HALO = 2 * HS + 2 * HR
UNIT = 8
Z_SIZE = 8
UNITS = ROWS // UNIT
F32 = jnp.float32
BF16 = jnp.bfloat16
MESH = pl.DeviceIdType.MESH
cat = jnp.concatenate


def kernel(probes_hbm, blocks_hbm, col, send_sub, send_reg, coeffs, total,
           probes, raw, weights, state, landing, outgoing, cheb,
           in_sem, send_sem, recv_sem):
    region = lax.axis_index("region")
    sub = lax.axis_index("sub")
    last_region = lax.axis_size("region") - 1
    last_sub = lax.axis_size("sub") - 1
    links = (
        (0, HS, "sub", sub + 1, sub < last_sub, sub > 0),
        (HS, HS, "sub", sub - 1, sub > 0, sub < last_sub),
        (2 * HS, HR, "region", region + 1, region < last_region, region > 0),
        (2 * HS + HR, HR, "region", region - 1, region > 0, region < last_region),
    )
    urgent = jnp.where(lax.rem(sub, Z_SIZE) == 0, 1, 0)

    def load_rows(u):
        rows = pl.ds(u * UNIT, UNIT)
        return pltpu.make_async_copy(blocks_hbm.at[rows], raw.at[rows], in_sem.at[u])

    probes_copy = pltpu.make_async_copy(probes_hbm, probes, in_sem.at[UNITS])
    probes_copy.start()
    barrier = pltpu.get_barrier_semaphore()
    for _, _, axis, target, sends, _ in links:
        @pl.when(sends)
        def _():
            pl.semaphore_signal(barrier, inc=1, device_id={axis: target}, device_id_type=MESH)
    for u in range(UNITS):
        load_rows(u).start()

    def sub_list(which):
        return [(HS * which + i, jnp.maximum(send_sub[0, 1 - which, i], 0)) for i in range(HS)]

    first_list = sub_list(urgent)
    second_list = sub_list(1 - urgent)
    third_list = [
        (2 * HS + HR * which + i, jnp.maximum(send_reg[0, 1 - which, i], 0)) for which in range(2) for i in range(HR)
    ]

    def halo_copy(step, link):
        first, count, axis, target, _, _ = links[link]
        slots = pl.ds(first, count)
        return pltpu.make_async_remote_copy(
            src_ref=outgoing.at[step, slots],
            dst_ref=landing.at[step, slots],
            send_sem=send_sem.at[step, link],
            recv_sem=recv_sem.at[step, link],
            device_id={axis: target},
            device_id_type=MESH,
        )

    def send(step, link, when=True):
        @pl.when(jnp.logical_and(links[link][4], when))
        def _():
            halo_copy(step, link).start()

    def take_halo(step):
        now = lax.rem(step, 2)
        for link, (first, count, _, _, _, arrives) in enumerate(links):
            @pl.when(arrives)
            def _():
                halo_copy(step, link).wait_recv()
                for slot in range(first, first + count):
                    state[now, ROWS + slot] = landing[step, slot]

    probes_copy.wait()
    for i in range(ROWS):
        state[0, i] = probes[:, i * BLK:(i + 1) * BLK]
    zero = jnp.zeros((PROBES, BLK), BF16)
    for slot in range(HALO):
        for now in range(2):
            state[now, ROWS + slot] = zero
    for slot, row in first_list + second_list + third_list:
        outgoing[0, slot] = state[0, row]
    peers = sum(jnp.where(sends, 1, 0) for _, _, _, _, sends, _ in links)
    pl.semaphore_wait(barrier, peers)
    for link in range(4):
        send(0, link)
    first_coeff = coeffs[0]
    for i in range(ROWS):
        wide = probes[:, i * BLK:(i + 1) * BLK].astype(F32)
        cheb[0, i] = wide
        cheb[1, i] = jnp.zeros_like(wide)
        total[:, i * BLK:(i + 1) * BLK] = first_coeff * wide

    def transpose_unit(u, carry):
        load_rows(u).wait()
        for i in range(UNIT):
            for k in range(NNZ):
                weights[u * UNIT + i, k] = raw[u * UNIT + i, k].T
        return carry

    lax.fori_loop(0, UNITS, transpose_unit, 0)

    def push_own(rows, m, staged):
        r = rows[4 * m:4 * m + 4]
        rhs = cat([cat([weights[r[a], 0], weights[r[a + 1], 0]], 1) for a in (0, 2)], 0)
        pltpu.matmul_push_rhs(rhs, staged, m)

    def push_others(rows, m, pair):
        a, b = rows[4 * m + 2 * pair:4 * m + 2 * pair + 2]
        rhs = cat([cat([weights[a, k], weights[b, k]], 1) for k in (1, 2)], 0)
        pltpu.matmul_push_rhs(rhs, pair, m)

    def multiply_own(now, rows, m, accs, staged):
        v = [state[now, row] for row in rows[4 * m:4 * m + 4]]
        pltpu.matmul_acc_lhs(accs[m][0], cat([cat([v[0], zero], 1), cat([v[1], zero], 1)], 0), staged)
        pltpu.matmul_acc_lhs(accs[m][1], cat([cat([zero, v[2]], 1), cat([zero, v[3]], 1)], 0))

    def multiply_others(now, rows, m, pair, accs):
        lhs = [cat([state[now, col[k, row]] for k in (1, 2)], 1) for row in rows[4 * m + 2 * pair:4 * m + 2 * pair + 2]]
        pltpu.matmul_acc_lhs(accs[m][pair], cat(lhs, 0), pair)

    def issue_others(now, rows, accs):
        for pair in range(2):
            for m in range(2):
                push_others(rows, m, pair)
                multiply_others(now, rows, m, pair, accs)

    def issue_own(now, rows, accs, staged=0):
        for m in range(2):
            push_own(rows, m, staged)
            multiply_own(now, rows, m, accs, staged)

    def issue(now, rows, accs):
        for pair in range(2):
            for m in range(2):
                push_others(rows, m, pair)
                multiply_others(now, rows, m, pair, accs)
        issue_own(now, rows, accs)

    def products(accs):
        result = []
        for m in range(2):
            for half in range(2):
                both = pltpu.matmul_pop(accs[m][half])
                result.append(both[:PROBES, :BLK])
                result.append(both[PROBES:, BLK:])
        return result

    def unit_rows(unit):
        return [unit * UNIT + i for i in range(UNIT)]

    def run(*a):
        sets = (((a[0], a[1]), (a[2], a[3])), ((a[4], a[5]), (a[6], a[7])))

        def one_step(step, carry):
            now = lax.rem(step, 2)
            later = 1 - now
            scale = jnp.where(step == 0, 1.0, 2.0).astype(F32)
            coeff = coeffs[step + 1]

            def finish_list(slots, accs):
                for (slot, row), product in zip(slots, products(accs)):
                    outgoing[step + 1, slot] = (scale * product - cheb[later, row]).astype(BF16)

            def finish(unit, accs):
                for row, product in zip(unit_rows(unit), products(accs)):
                    new = scale * product - cheb[later, row]
                    cheb[later, row] = new
                    state[later, row] = new.astype(BF16)
                    total[:, row * BLK:(row + 1) * BLK] += coeff * new

            rows = [row for _, row in first_list]
            issue_own(now, rows, sets[0])
            for pair in range(2):
                for m in range(2):
                    push_others(rows, m, pair)
            take_halo(step)
            for pair in range(2):
                for m in range(2):
                    multiply_others(now, rows, m, pair, sets[0])
            finish_list(first_list, sets[0])
            send(step + 1, 0, urgent == 0)
            send(step + 1, 1, urgent == 1)
            issue(now, [row for _, row in second_list], sets[1])
            issue(now, [row for _, row in third_list], sets[0])
            finish_list(second_list, sets[1])
            send(step + 1, 0, urgent == 1)
            send(step + 1, 1, urgent == 0)
            for unit in range(UNITS):
                issue(now, unit_rows(unit), sets[(unit + 1) % 2])
                if unit:
                    finish(unit - 1, sets[unit % 2])
                else:
                    finish_list(third_list, sets[0])
                    send(step + 1, 2)
                    send(step + 1, 3)
            finish(UNITS - 1, sets[UNITS % 2])
            return carry

        lax.fori_loop(0, DEG - 1, one_step, 0)

        now = (DEG - 1) % 2
        coeff = coeffs[DEG]

        def finish_own(unit, accs):
            for row, product in zip(unit_rows(unit), products(accs)):
                total[:, row * BLK:(row + 1) * BLK] += coeff * (2.0 * product - cheb[1 - now, row])

        def finish_last(unit, accs):
            for row, product in zip(unit_rows(unit), products(accs)):
                total[:, row * BLK:(row + 1) * BLK] += coeff * (2.0 * product)

        for unit in range(UNITS):
            issue_own(now, unit_rows(unit), sets[unit % 2], unit % 2)
            if unit:
                finish_own(unit - 1, sets[(unit - 1) % 2])
        finish_own(UNITS - 1, sets[(UNITS - 1) % 2])
        take_halo(DEG - 1)
        for unit in range(UNITS):
            issue_others(now, unit_rows(unit), sets[unit % 2])
            if unit:
                finish_last(unit - 1, sets[(unit - 1) % 2])
        finish_last(UNITS - 1, sets[(UNITS - 1) % 2])

    pl.run_scoped(run, *[pltpu.ACC(mxu_id=m)((2 * PROBES, 2 * BLK), F32) for m in (0, 0, 1, 1, 0, 0, 1, 1)])

    def sent(step, carry):
        for link in range(4):
            @pl.when(links[link][4])
            def _():
                halo_copy(step, link).wait_send()
        return carry

    lax.fori_loop(0, DEG, sent, 0)


def local(probes, blocks, col_slot, send_sub, send_reg, coeffs):
    in_hbm = pl.BlockSpec(memory_space=pltpu.HBM)
    scalar = pl.BlockSpec(memory_space=pltpu.SMEM)
    width = ROWS * BLK
    args = (probes, blocks, col_slot.T, send_sub, send_reg, coeffs)
    return pl.pallas_call(
        kernel,
        out_shape=jax.ShapeDtypeStruct((PROBES, width), F32),
        in_specs=[in_hbm, in_hbm, scalar, scalar, scalar, scalar],
        out_specs=pl.BlockSpec(memory_space=pltpu.VMEM),
        scratch_shapes=[
            pltpu.VMEM((PROBES, width), BF16),
            pltpu.VMEM((ROWS, NNZ, BLK, BLK), BF16),
            pltpu.VMEM((ROWS, NNZ, BLK, BLK), BF16),
            pltpu.VMEM((2, ROWS + HALO, PROBES, BLK), BF16),
            pltpu.VMEM((DEG, HALO, PROBES, BLK), BF16),
            pltpu.VMEM((DEG, HALO, PROBES, BLK), BF16),
            pltpu.VMEM((2, ROWS, PROBES, BLK), F32),
            pltpu.SemaphoreType.DMA((UNITS + 1,)),
            pltpu.SemaphoreType.DMA((DEG, 4)),
            pltpu.SemaphoreType.DMA((DEG, 4)),
        ],
        compiler_params=pltpu.CompilerParams(
            collective_id=0, has_side_effects=True, vmem_limit_bytes=40 << 20
        ),
    )(*(pltpu.with_memory_space_constraint(x, pltpu.HBM) for x in args))


def solution(mesh):
    both = ("region", "sub")
    mapped = jax.shard_map(
        local,
        mesh=mesh,
        in_specs=(
            P(None, both),
            P(both, None, None, None),
            P(both, None),
            P(both, None, None),
            P(both, None, None),
            P(),
        ),
        out_specs=P(None, both),
        check_vma=False,
    )

    def run(*args):
        with jax.sharding.use_abstract_mesh(mesh.abstract_mesh):
            return mapped(*args)

    return run
```

time: 60.1 us -> 46 us (0.77)
  the two profiles are of different devices: /device:TPU:8 before, /device:TPU:6 now
where the time goes in v1:
time: 46 us; the launch traced here: 45.8 us
  Pallas kernels  44.6 us (97%)
  local copies, waits for them, and re-layouts  1.19 us (3%)
    pallas_call x1, Pallas kernels, local(): pl.pallas_call(kernel, out_shape=jax.ShapeDtypeStruct((PROBES, width), F3...  44.6 us
    unnamed x1, local copies, waits for them, and re-layouts  1.19 us

profile of v1, /device:TPU:6, one launch (start us, length us, event | category | flops | bytes accessed | tf_op | source)
XLA Modules:
  0.0 45.8 jit_solution(7249620466212020227)
XLA Ops:
  0.0 44.6 %shard_map.64 = f32[32,13312]{1,0:T(8,128)S(1)} custom-call(bf16[32,13312]{1,0:T(8,128)(2,1)} %probes_hbm.1, bf16[104,3,128,128]{3,2,1,0:T(8,128)(2,1)} %blocks_hbm.1, s32[3,104]{1,0:T(4,128)} %bitcast.1, s32[1,2,8]{2,1,0:T(2,128)} %send_sub.1, s32[1,2,4]{2,1,0:T(2,128)} %send_reg.1, f32[9]{0:T(128)} %coeffs.1), custom_call_target="tpu_custom_call" | custom-call | tf_op jit(solution)/shard_map/pallas_call | solution.py:257
  44.7 1.2 %copy.8 = f32[32,13312]{1,0:T(8,128)} copy(f32[32,13312]{1,0:T(8,128)S(1)} %shard_map.64) | data formatting | bytes 3407872

commit v2 on v1

--- a/solution.py
+++ b/solution.py
@@ -22,9 +22,9 @@
 cat = jnp.concatenate
 
 
-def kernel(probes_hbm, blocks_hbm, col, send_sub, send_reg, coeffs, total,
+def kernel(probes_hbm, blocks_hbm, col_hbm, sub_hbm, reg_hbm, coeffs_hbm, total,
            probes, raw, weights, state, landing, outgoing, cheb,
-           in_sem, send_sem, recv_sem):
+           col, send_sub, send_reg, coeffs, in_sem, table_sem, send_sem, recv_sem):
     region = lax.axis_index("region")
     sub = lax.axis_index("sub")
     last_region = lax.axis_size("region") - 1
@@ -41,15 +41,19 @@
         rows = pl.ds(u * UNIT, UNIT)
         return pltpu.make_async_copy(blocks_hbm.at[rows], raw.at[rows], in_sem.at[u])
 
-    probes_copy = pltpu.make_async_copy(probes_hbm, probes, in_sem.at[UNITS])
-    probes_copy.start()
     barrier = pltpu.get_barrier_semaphore()
     for _, _, axis, target, sends, _ in links:
         @pl.when(sends)
         def _():
             pl.semaphore_signal(barrier, inc=1, device_id={axis: target}, device_id_type=MESH)
-    for u in range(UNITS):
-        load_rows(u).start()
+    probes_copy = pltpu.make_async_copy(probes_hbm, probes, in_sem.at[UNITS])
+    probes_copy.start()
+    tables = ((sub_hbm, send_sub), (reg_hbm, send_reg), (col_hbm, col), (coeffs_hbm, coeffs))
+    table_copies = [pltpu.make_async_copy(src, dst, table_sem.at[i]) for i, (src, dst) in enumerate(tables)]
+    for copy in table_copies:
+        copy.start()
+    table_copies[0].wait()
+    table_copies[1].wait()
 
     def sub_list(which):
         return [(HS * which + i, jnp.maximum(send_sub[0, 1 - which, i], 0)) for i in range(HS)]
@@ -77,28 +81,45 @@
         def _():
             halo_copy(step, link).start()
 
+    def send_sub_link(step, which):
+        send(step, 0, which == 0)
+        send(step, 1, which == 1)
+
+    def take_link(step, link, when=True):
+        first, count, _, _, _, arrives = links[link]
+
+        @pl.when(jnp.logical_and(arrives, when))
+        def _():
+            halo_copy(step, link).wait_recv()
+            for slot in range(first, first + count):
+                state[lax.rem(step, 2), ROWS + slot] = landing[step, slot]
+
     def take_halo(step):
-        now = lax.rem(step, 2)
-        for link, (first, count, _, _, _, arrives) in enumerate(links):
-            @pl.when(arrives)
-            def _():
-                halo_copy(step, link).wait_recv()
-                for slot in range(first, first + count):
-                    state[now, ROWS + slot] = landing[step, slot]
-
-    probes_copy.wait()
-    for i in range(ROWS):
-        state[0, i] = probes[:, i * BLK:(i + 1) * BLK]
+        take_link(step, 2)
+        take_link(step, 3)
+        take_link(step, 0, urgent == 0)
+        take_link(step, 1)
+        take_link(step, 0, urgent == 1)
+
     zero = jnp.zeros((PROBES, BLK), BF16)
     for slot in range(HALO):
         for now in range(2):
             state[now, ROWS + slot] = zero
+    probes_copy.wait()
+    for u in range(UNITS):
+        load_rows(u).start()
+    for i in range(ROWS):
+        state[0, i] = probes[:, i * BLK:(i + 1) * BLK]
+    peers = sum(jnp.where(sends, 1, 0) for _, _, _, _, sends, _ in links)
     for slot, row in first_list + second_list + third_list:
         outgoing[0, slot] = state[0, row]
-    peers = sum(jnp.where(sends, 1, 0) for _, _, _, _, sends, _ in links)
     pl.semaphore_wait(barrier, peers)
-    for link in range(4):
-        send(0, link)
+    send_sub_link(0, urgent)
+    send_sub_link(0, 1 - urgent)
+    send(0, 2)
+    send(0, 3)
+    table_copies[2].wait()
+    table_copies[3].wait()
     first_coeff = coeffs[0]
     for i in range(ROWS):
         wide = probes[:, i * BLK:(i + 1) * BLK].astype(F32)
@@ -130,26 +151,37 @@
         pltpu.matmul_acc_lhs(accs[m][0], cat([cat([v[0], zero], 1), cat([v[1], zero], 1)], 0), staged)
         pltpu.matmul_acc_lhs(accs[m][1], cat([cat([zero, v[2]], 1), cat([zero, v[3]], 1)], 0))
 
-    def multiply_others(now, rows, m, pair, accs):
-        lhs = [cat([state[now, col[k, row]] for k in (1, 2)], 1) for row in rows[4 * m + 2 * pair:4 * m + 2 * pair + 2]]
+    def columns(rows):
+        return [(col[1, row], col[2, row]) for row in rows]
+
+    def multiply_others(now, taken, m, pair, accs):
+        lhs = [cat([state[now, c] for c in both], 1) for both in taken[4 * m + 2 * pair:4 * m + 2 * pair + 2]]
         pltpu.matmul_acc_lhs(accs[m][pair], cat(lhs, 0), pair)
 
     def issue_others(now, rows, accs):
+        taken = columns(rows)
         for pair in range(2):
             for m in range(2):
                 push_others(rows, m, pair)
-                multiply_others(now, rows, m, pair, accs)
+                multiply_others(now, taken, m, pair, accs)
 
     def issue_own(now, rows, accs, staged=0):
         for m in range(2):
             push_own(rows, m, staged)
             multiply_own(now, rows, m, accs, staged)
 
-    def issue(now, rows, accs):
+    def stage_others(rows):
         for pair in range(2):
             for m in range(2):
                 push_others(rows, m, pair)
-                multiply_others(now, rows, m, pair, accs)
+
+    def multiply_staged(now, taken, accs):
+        for pair in range(2):
+            for m in range(2):
+                multiply_others(now, taken, m, pair, accs)
+
+    def issue(now, rows, accs):
+        issue_others(now, rows, accs)
         issue_own(now, rows, accs)
 
     def products(accs):
@@ -186,21 +218,16 @@
 
             rows = [row for _, row in first_list]
             issue_own(now, rows, sets[0])
-            for pair in range(2):
-                for m in range(2):
-                    push_others(rows, m, pair)
+            stage_others(rows)
+            taken = columns(rows)
             take_halo(step)
-            for pair in range(2):
-                for m in range(2):
-                    multiply_others(now, rows, m, pair, sets[0])
+            multiply_staged(now, taken, sets[0])
             finish_list(first_list, sets[0])
-            send(step + 1, 0, urgent == 0)
-            send(step + 1, 1, urgent == 1)
+            send_sub_link(step + 1, urgent)
             issue(now, [row for _, row in second_list], sets[1])
             issue(now, [row for _, row in third_list], sets[0])
             finish_list(second_list, sets[1])
-            send(step + 1, 0, urgent == 1)
-            send(step + 1, 1, urgent == 0)
+            send_sub_link(step + 1, 1 - urgent)
             for unit in range(UNITS):
                 issue(now, unit_rows(unit), sets[(unit + 1) % 2])
                 if unit:
@@ -230,10 +257,13 @@
             if unit:
                 finish_own(unit - 1, sets[(unit - 1) % 2])
         finish_own(UNITS - 1, sets[(UNITS - 1) % 2])
+        stage_others(unit_rows(0))
+        taken = columns(unit_rows(0))
         take_halo(DEG - 1)
+        multiply_staged(now, taken, sets[0])
         for unit in range(UNITS):
-            issue_others(now, unit_rows(unit), sets[unit % 2])
             if unit:
+                issue_others(now, unit_rows(unit), sets[unit % 2])
                 finish_last(unit - 1, sets[(unit - 1) % 2])
         finish_last(UNITS - 1, sets[(UNITS - 1) % 2])
 
@@ -251,13 +281,12 @@
 
 def local(probes, blocks, col_slot, send_sub, send_reg, coeffs):
     in_hbm = pl.BlockSpec(memory_space=pltpu.HBM)
-    scalar = pl.BlockSpec(memory_space=pltpu.SMEM)
     width = ROWS * BLK
     args = (probes, blocks, col_slot.T, send_sub, send_reg, coeffs)
     return pl.pallas_call(
         kernel,
         out_shape=jax.ShapeDtypeStruct((PROBES, width), F32),
-        in_specs=[in_hbm, in_hbm, scalar, scalar, scalar, scalar],
+        in_specs=[in_hbm] * 6,
         out_specs=pl.BlockSpec(memory_space=pltpu.VMEM),
         scratch_shapes=[
             pltpu.VMEM((PROBES, width), BF16),
@@ -267,7 +296,12 @@
             pltpu.VMEM((DEG, HALO, PROBES, BLK), BF16),
             pltpu.VMEM((DEG, HALO, PROBES, BLK), BF16),
             pltpu.VMEM((2, ROWS, PROBES, BLK), F32),
+            pltpu.SMEM((NNZ, ROWS), jnp.int32),
+            pltpu.SMEM((1, 2, HS), jnp.int32),
+            pltpu.SMEM((1, 2, HR), jnp.int32),
+            pltpu.SMEM((DEG + 1,), F32),
             pltpu.SemaphoreType.DMA((UNITS + 1,)),
+            pltpu.SemaphoreType.DMA((4,)),
             pltpu.SemaphoreType.DMA((DEG, 4)),
             pltpu.SemaphoreType.DMA((DEG, 4)),
         ],

time: 46 us -> 45 us (0.978)
  Pallas kernels: 44.6 us -> 43.8 us
    pallas_call x1, Pallas kernels: 44.6 us -> 43.8 us  [local(): pl.pallas_call(kernel, out_shape=jax.ShapeDtypeStruct((PROBES, width), F3...]
where the time goes in v2:
time: 45 us
  Pallas kernels  43.8 us (97%)
  local copies, waits for them, and re-layouts  1.19 us (3%)
    pallas_call x1, Pallas kernels, local(): pl.pallas_call(kernel, out_shape=jax.ShapeDtypeStruct((PROBES, width), F3...  43.8 us
    unnamed x1, local copies, waits for them, and re-layouts  1.19 us

profile of v2, /device:TPU:6, one launch (start us, length us, event | category | flops | bytes accessed | tf_op | source)
XLA Modules:
  0.0 45.0 jit_solution(2564514516117915425)
XLA Ops:
  0.0 43.8 %shard_map.64 = f32[32,13312]{1,0:T(8,128)S(1)} custom-call(bf16[32,13312]{1,0:T(8,128)(2,1)} %probes_hbm.1, bf16[104,3,128,128]{3,2,1,0:T(8,128)(2,1)} %blocks_hbm.1, s32[3,104]{1,0:T(4,128)} %bitcast.1, s32[1,2,8]{2,1,0:T(2,128)} %sub_hbm.1, s32[1,2,4]{2,1,0:T(2,128)} %reg_hbm.1, f32[9]{0:T(128)} %coeffs_hbm.1), custom_call_target="tpu_custom_call" | custom-call | tf_op jit(solution)/shard_map/pallas_call | solution.py:286
  43.8 1.2 %copy.8 = f32[32,13312]{1,0:T(8,128)} copy(f32[32,13312]{1,0:T(8,128)S(1)} %shard_map.64) | data formatting | bytes 3407872

commit v3 on v2

--- a/solution.py
+++ b/solution.py
@@ -15,6 +15,8 @@
 HALO = 2 * HS + 2 * HR
 UNIT = 8
 Z_SIZE = 8
+GROUPS = 2
+PART = PROBES // GROUPS
 UNITS = ROWS // UNIT
 F32 = jnp.float32
 BF16 = jnp.bfloat16
@@ -23,7 +25,7 @@
 
 
 def kernel(probes_hbm, blocks_hbm, col_hbm, sub_hbm, reg_hbm, coeffs_hbm, total,
-           probes, raw, weights, state, landing, outgoing, cheb,
+           probes, raw, weights, state, land_sub, land_reg, out_sub, out_reg, cheb,
            col, send_sub, send_reg, coeffs, in_sem, table_sem, send_sem, recv_sem):
     region = lax.axis_index("region")
     sub = lax.axis_index("sub")
@@ -60,46 +62,64 @@
 
     first_list = sub_list(urgent)
     second_list = sub_list(1 - urgent)
-    third_list = [
-        (2 * HS + HR * which + i, jnp.maximum(send_reg[0, 1 - which, i], 0)) for which in range(2) for i in range(HR)
-    ]
-
-    def halo_copy(step, link):
+    third_list = [(HR * which + i, jnp.maximum(send_reg[0, 1 - which, i], 0)) for which in range(2) for i in range(HR)]
+
+    def message(step, link, group=0):
         first, count, axis, target, _, _ = links[link]
-        slots = pl.ds(first, count)
+        if link < 2:
+            slots = pl.ds(first, count)
+            src, dst, which = out_sub.at[step, group, slots], land_sub.at[step, group, slots], GROUPS * link + group
+        else:
+            slots = pl.ds(first - 2 * HS, count)
+            src, dst, which = out_reg.at[step, slots], land_reg.at[step, slots], 2 * GROUPS + link - 2
         return pltpu.make_async_remote_copy(
-            src_ref=outgoing.at[step, slots],
-            dst_ref=landing.at[step, slots],
-            send_sem=send_sem.at[step, link],
-            recv_sem=recv_sem.at[step, link],
+            src_ref=src,
+            dst_ref=dst,
+            send_sem=send_sem.at[step, which],
+            recv_sem=recv_sem.at[step, which],
             device_id={axis: target},
             device_id_type=MESH,
         )
 
-    def send(step, link, when=True):
-        @pl.when(jnp.logical_and(links[link][4], when))
-        def _():
-            halo_copy(step, link).start()
-
-    def send_sub_link(step, which):
-        send(step, 0, which == 0)
-        send(step, 1, which == 1)
-
-    def take_link(step, link, when=True):
-        first, count, _, _, _, arrives = links[link]
-
-        @pl.when(jnp.logical_and(arrives, when))
-        def _():
-            halo_copy(step, link).wait_recv()
-            for slot in range(first, first + count):
-                state[lax.rem(step, 2), ROWS + slot] = landing[step, slot]
-
-    def take_halo(step):
-        take_link(step, 2)
-        take_link(step, 3)
-        take_link(step, 0, urgent == 0)
-        take_link(step, 1)
-        take_link(step, 0, urgent == 1)
+    def send_reg_links(step):
+        for link in (2, 3):
+            @pl.when(links[link][4])
+            def _():
+                message(step, link).start()
+
+    def send_sub_link(step, which, group):
+        for link in range(2):
+            @pl.when(jnp.logical_and(links[link][4], which == link))
+            def _():
+                message(step, link, group).start()
+
+    def take_reg_links(step):
+        for link in (2, 3):
+            first, count, _, _, _, arrives = links[link]
+
+            @pl.when(arrives)
+            def _():
+                message(step, link).wait_recv()
+                for slot in range(first, first + count):
+                    state[lax.rem(step, 2), ROWS + slot] = land_reg[step, slot - 2 * HS]
+
+    def take_sub_link(step, which, group):
+        for link in range(2):
+            first, count, _, _, _, arrives = links[link]
+
+            @pl.when(jnp.logical_and(arrives, which == link))
+            def _():
+                message(step, link, group).wait_recv()
+                for slot in range(first, first + count):
+                    state[lax.rem(step, 2), ROWS + slot, part(group)] = land_sub[step, group, slot]
+
+    def part(group):
+        return slice(group * PART, (group + 1) * PART)
+
+    def take_early(step):
+        take_reg_links(step)
+        for group in range(GROUPS):
+            take_sub_link(step, urgent, group)
 
     zero = jnp.zeros((PROBES, BLK), BF16)
     for slot in range(HALO):
@@ -111,13 +131,16 @@
     for i in range(ROWS):
         state[0, i] = probes[:, i * BLK:(i + 1) * BLK]
     peers = sum(jnp.where(sends, 1, 0) for _, _, _, _, sends, _ in links)
-    for slot, row in first_list + second_list + third_list:
-        outgoing[0, slot] = state[0, row]
+    for slot, row in first_list + second_list:
+        for group in range(GROUPS):
+            out_sub[0, group, slot] = state[0, row, part(group)]
+    for slot, row in third_list:
+        out_reg[0, slot] = state[0, row]
     pl.semaphore_wait(barrier, peers)
-    send_sub_link(0, urgent)
-    send_sub_link(0, 1 - urgent)
-    send(0, 2)
-    send(0, 3)
+    for which in (urgent, 1 - urgent):
+        for group in range(GROUPS):
+            send_sub_link(0, which, group)
+    send_reg_links(0)
     table_copies[2].wait()
     table_copies[3].wait()
     first_coeff = coeffs[0]
@@ -180,24 +203,48 @@
             for m in range(2):
                 multiply_others(now, taken, m, pair, accs)
 
+    small_zero = jnp.zeros((PART, BLK), BF16)
+
+    def issue_own_groups(now, rows, groups):
+        for m in range(2):
+            push_own(rows, m, 0)
+            staged = 0
+            for group in range(GROUPS):
+                v = [state[now, row, part(group)] for row in rows[4 * m:4 * m + 4]]
+                upper = cat([cat([v[0], small_zero], 1), cat([v[1], small_zero], 1)], 0)
+                lower = cat([cat([small_zero, v[2]], 1), cat([small_zero, v[3]], 1)], 0)
+                pltpu.matmul_acc_lhs(groups[group][m][0], upper, staged)
+                pltpu.matmul_acc_lhs(groups[group][m][1], lower)
+                staged = None
+
+    def multiply_group(now, taken, group, accs):
+        for pair in range(2):
+            for m in range(2):
+                lhs = [
+                    cat([state[now, c, part(group)] for c in both], 1)
+                    for both in taken[4 * m + 2 * pair:4 * m + 2 * pair + 2]
+                ]
+                pltpu.matmul_acc_lhs(accs[m][pair], cat(lhs, 0), pair)
+
     def issue(now, rows, accs):
         issue_others(now, rows, accs)
         issue_own(now, rows, accs)
 
-    def products(accs):
+    def products(accs, count=PROBES):
         result = []
         for m in range(2):
             for half in range(2):
                 both = pltpu.matmul_pop(accs[m][half])
-                result.append(both[:PROBES, :BLK])
-                result.append(both[PROBES:, BLK:])
+                result.append(both[:count, :BLK])
+                result.append(both[count:, BLK:])
         return result
 
     def unit_rows(unit):
         return [unit * UNIT + i for i in range(UNIT)]
 
     def run(*a):
-        sets = (((a[0], a[1]), (a[2], a[3])), ((a[4], a[5]), (a[6], a[7])))
+        quads = [((a[i], a[i + 1]), (a[i + 2], a[i + 3])) for i in range(0, len(a), 4)]
+        sets, groups = quads[:2], quads[2:]
 
         def one_step(step, carry):
             now = lax.rem(step, 2)
@@ -205,9 +252,20 @@
             scale = jnp.where(step == 0, 1.0, 2.0).astype(F32)
             coeff = coeffs[step + 1]
 
-            def finish_list(slots, accs):
-                for (slot, row), product in zip(slots, products(accs)):
-                    outgoing[step + 1, slot] = (scale * product - cheb[later, row]).astype(BF16)
+            def finish_urgent(group, accs):
+                for (slot, row), product in zip(first_list, products(accs, PART)):
+                    new = scale * product - cheb[later, row, part(group)]
+                    out_sub[step + 1, group, slot] = new.astype(BF16)
+
+            def finish_second(accs):
+                for (slot, row), product in zip(second_list, products(accs)):
+                    new = (scale * product - cheb[later, row]).astype(BF16)
+                    for group in range(GROUPS):
+                        out_sub[step + 1, group, slot] = new[part(group)]
+
+            def finish_third(accs):
+                for (slot, row), product in zip(third_list, products(accs)):
+                    out_reg[step + 1, slot] = (scale * product - cheb[later, row]).astype(BF16)
 
             def finish(unit, accs):
                 for row, product in zip(unit_rows(unit), products(accs)):
@@ -217,25 +275,29 @@
                     total[:, row * BLK:(row + 1) * BLK] += coeff * new
 
             rows = [row for _, row in first_list]
-            issue_own(now, rows, sets[0])
+            issue_own_groups(now, rows, groups)
             stage_others(rows)
             taken = columns(rows)
-            take_halo(step)
-            multiply_staged(now, taken, sets[0])
-            finish_list(first_list, sets[0])
-            send_sub_link(step + 1, urgent)
+            take_early(step)
+            for group in range(GROUPS):
+                take_sub_link(step, 1 - urgent, group)
+                multiply_group(now, taken, group, groups[group])
+                if group + 1 < GROUPS:
+                    stage_others(rows)
+                finish_urgent(group, groups[group])
+                send_sub_link(step + 1, urgent, group)
             issue(now, [row for _, row in second_list], sets[1])
             issue(now, [row for _, row in third_list], sets[0])
-            finish_list(second_list, sets[1])
-            send_sub_link(step + 1, 1 - urgent)
+            finish_second(sets[1])
+            for group in range(GROUPS):
+                send_sub_link(step + 1, 1 - urgent, group)
             for unit in range(UNITS):
                 issue(now, unit_rows(unit), sets[(unit + 1) % 2])
                 if unit:
                     finish(unit - 1, sets[unit % 2])
                 else:
-                    finish_list(third_list, sets[0])
-                    send(step + 1, 2)
-                    send(step + 1, 3)
+                    finish_third(sets[0])
+                    send_reg_links(step + 1)
             finish(UNITS - 1, sets[UNITS % 2])
             return carry
 
@@ -259,7 +321,9 @@
         finish_own(UNITS - 1, sets[(UNITS - 1) % 2])
         stage_others(unit_rows(0))
         taken = columns(unit_rows(0))
-        take_halo(DEG - 1)
+        take_early(DEG - 1)
+        for group in range(GROUPS):
+            take_sub_link(DEG - 1, 1 - urgent, group)
         multiply_staged(now, taken, sets[0])
         for unit in range(UNITS):
             if unit:
@@ -267,13 +331,15 @@
                 finish_last(unit - 1, sets[(unit - 1) % 2])
         finish_last(UNITS - 1, sets[(UNITS - 1) % 2])
 
-    pl.run_scoped(run, *[pltpu.ACC(mxu_id=m)((2 * PROBES, 2 * BLK), F32) for m in (0, 0, 1, 1, 0, 0, 1, 1)])
+    heights = (2 * PROBES,) * 2 + (2 * PART,) * GROUPS
+    pl.run_scoped(run, *[pltpu.ACC(mxu_id=m)((height, 2 * BLK), F32) for height in heights for m in (0, 0, 1, 1)])
 
     def sent(step, carry):
         for link in range(4):
-            @pl.when(links[link][4])
-            def _():
-                halo_copy(step, link).wait_send()
+            for group in range(GROUPS if link < 2 else 1):
+                @pl.when(links[link][4])
+                def _():
+                    message(step, link, group).wait_send()
         return carry
 
     lax.fori_loop(0, DEG, sent, 0)
@@ -293,8 +359,10 @@
             pltpu.VMEM((ROWS, NNZ, BLK, BLK), BF16),
             pltpu.VMEM((ROWS, NNZ, BLK, BLK), BF16),
             pltpu.VMEM((2, ROWS + HALO, PROBES, BLK), BF16),
-            pltpu.VMEM((DEG, HALO, PROBES, BLK), BF16),
-            pltpu.VMEM((DEG, HALO, PROBES, BLK), BF16),
+            pltpu.VMEM((DEG, GROUPS, 2 * HS, PART, BLK), BF16),
+            pltpu.VMEM((DEG, 2 * HR, PROBES, BLK), BF16),
+            pltpu.VMEM((DEG, GROUPS, 2 * HS, PART, BLK), BF16),
+            pltpu.VMEM((DEG, 2 * HR, PROBES, BLK), BF16),
             pltpu.VMEM((2, ROWS, PROBES, BLK), F32),
             pltpu.SMEM((NNZ, ROWS), jnp.int32),
             pltpu.SMEM((1, 2, HS), jnp.int32),
@@ -302,8 +370,8 @@
             pltpu.SMEM((DEG + 1,), F32),
             pltpu.SemaphoreType.DMA((UNITS + 1,)),
             pltpu.SemaphoreType.DMA((4,)),
-            pltpu.SemaphoreType.DMA((DEG, 4)),
-            pltpu.SemaphoreType.DMA((DEG, 4)),
+            pltpu.SemaphoreType.DMA((DEG, 2 * GROUPS + 2)),
+            pltpu.SemaphoreType.DMA((DEG, 2 * GROUPS + 2)),
         ],
         compiler_params=pltpu.CompilerParams(
             collective_id=0, has_side_effects=True, vmem_limit_bytes=40 << 20

time: 45 us -> 43.8 us (0.973)
  Pallas kernels: 43.8 us -> 42.5 us
    pallas_call x1, Pallas kernels: 43.8 us -> 42.5 us  [local(): pl.pallas_call(kernel, out_shape=jax.ShapeDtypeStruct((PROBES, width), F3...]
where the time goes in v3:
time: 43.8 us; the launch traced here: 43.7 us
  Pallas kernels  42.5 us (97%)
  local copies, waits for them, and re-layouts  1.19 us (3%)
    pallas_call x1, Pallas kernels, local(): pl.pallas_call(kernel, out_shape=jax.ShapeDtypeStruct((PROBES, width), F3...  42.5 us
    unnamed x1, local copies, waits for them, and re-layouts  1.19 us

profile of v3, /device:TPU:6, one launch (start us, length us, event | category | flops | bytes accessed | tf_op | source)
XLA Modules:
  0.0 43.7 jit_solution(14016047772212658002)
XLA Ops:
  0.0 42.5 %shard_map.64 = f32[32,13312]{1,0:T(8,128)S(1)} custom-call(bf16[32,13312]{1,0:T(8,128)(2,1)} %probes_hbm.1, bf16[104,3,128,128]{3,2,1,0:T(8,128)(2,1)} %blocks_hbm.1, s32[3,104]{1,0:T(4,128)} %bitcast.1, s32[1,2,8]{2,1,0:T(2,128)} %sub_hbm.1, s32[1,2,4]{2,1,0:T(2,128)} %reg_hbm.1, f32[9]{0:T(128)} %coeffs_hbm.1), custom_call_target="tpu_custom_call" | custom-call | tf_op jit(solution)/shard_map/pallas_call | solution.py:352
  42.5 1.2 %copy.8 = f32[32,13312]{1,0:T(8,128)} copy(f32[32,13312]{1,0:T(8,128)S(1)} %shard_map.64) | data formatting | bytes 3407872

commit v4 on v3

--- a/solution.py
+++ b/solution.py
@@ -31,11 +31,11 @@
     sub = lax.axis_index("sub")
     last_region = lax.axis_size("region") - 1
     last_sub = lax.axis_size("sub") - 1
-    links = (
-        (0, HS, "sub", sub + 1, sub < last_sub, sub > 0),
-        (HS, HS, "sub", sub - 1, sub > 0, sub < last_sub),
-        (2 * HS, HR, "region", region + 1, region < last_region, region > 0),
-        (2 * HS + HR, HR, "region", region - 1, region > 0, region < last_region),
+    peers_at = (
+        ("sub", sub + 1, sub < last_sub),
+        ("sub", sub - 1, sub > 0),
+        ("region", region + 1, region < last_region),
+        ("region", region - 1, region > 0),
     )
     urgent = jnp.where(lax.rem(sub, Z_SIZE) == 0, 1, 0)
 
@@ -44,8 +44,8 @@
         return pltpu.make_async_copy(blocks_hbm.at[rows], raw.at[rows], in_sem.at[u])
 
     barrier = pltpu.get_barrier_semaphore()
-    for _, _, axis, target, sends, _ in links:
-        @pl.when(sends)
+    for axis, target, there in peers_at:
+        @pl.when(there)
         def _():
             pl.semaphore_signal(barrier, inc=1, device_id={axis: target}, device_id_type=MESH)
     probes_copy = pltpu.make_async_copy(probes_hbm, probes, in_sem.at[UNITS])
@@ -54,6 +54,8 @@
     table_copies = [pltpu.make_async_copy(src, dst, table_sem.at[i]) for i, (src, dst) in enumerate(tables)]
     for copy in table_copies:
         copy.start()
+    for u in range(UNITS):
+        load_rows(u).start()
     table_copies[0].wait()
     table_copies[1].wait()
 
@@ -64,14 +66,7 @@
     second_list = sub_list(1 - urgent)
     third_list = [(HR * which + i, jnp.maximum(send_reg[0, 1 - which, i], 0)) for which in range(2) for i in range(HR)]
 
-    def message(step, link, group=0):
-        first, count, axis, target, _, _ = links[link]
-        if link < 2:
-            slots = pl.ds(first, count)
-            src, dst, which = out_sub.at[step, group, slots], land_sub.at[step, group, slots], GROUPS * link + group
-        else:
-            slots = pl.ds(first - 2 * HS, count)
-            src, dst, which = out_reg.at[step, slots], land_reg.at[step, slots], 2 * GROUPS + link - 2
+    def remote_copy(src, dst, step, which, axis, target):
         return pltpu.make_async_remote_copy(
             src_ref=src,
             dst_ref=dst,
@@ -81,37 +76,47 @@
             device_id_type=MESH,
         )
 
+    def sub_message(step, link, group):
+        slots = pl.ds(HS * link, HS)
+        target = sub + 1 - 2 * link
+        return remote_copy(
+            out_sub.at[step, group, slots], land_sub.at[step, group, slots], step, GROUPS * link + group, "sub", target
+        )
+
+    def reg_message(step, link):
+        slots = pl.ds(HR * link, HR)
+        target = region + 1 - 2 * link
+        return remote_copy(out_reg.at[step, slots], land_reg.at[step, slots], step, 2 * GROUPS + link, "region", target)
+
+    def has_target(link, place, last):
+        return jnp.logical_or(jnp.logical_and(link == 0, place < last), jnp.logical_and(link == 1, place > 0))
+
     def send_reg_links(step):
-        for link in (2, 3):
-            @pl.when(links[link][4])
+        for link in range(2):
+            @pl.when(has_target(link, region, last_region))
             def _():
-                message(step, link).start()
-
-    def send_sub_link(step, which, group):
+                reg_message(step, link).start()
+
+    def send_sub_link(step, link, group):
+        @pl.when(has_target(link, sub, last_sub))
+        def _():
+            sub_message(step, link, group).start()
+
+    def take_reg_links(step):
         for link in range(2):
-            @pl.when(jnp.logical_and(links[link][4], which == link))
+            @pl.when(has_target(1 - link, region, last_region))
             def _():
-                message(step, link, group).start()
-
-    def take_reg_links(step):
-        for link in (2, 3):
-            first, count, _, _, _, arrives = links[link]
-
-            @pl.when(arrives)
-            def _():
-                message(step, link).wait_recv()
-                for slot in range(first, first + count):
-                    state[lax.rem(step, 2), ROWS + slot] = land_reg[step, slot - 2 * HS]
-
-    def take_sub_link(step, which, group):
-        for link in range(2):
-            first, count, _, _, _, arrives = links[link]
-
-            @pl.when(jnp.logical_and(arrives, which == link))
-            def _():
-                message(step, link, group).wait_recv()
-                for slot in range(first, first + count):
-                    state[lax.rem(step, 2), ROWS + slot, part(group)] = land_sub[step, group, slot]
+                reg_message(step, link).wait_recv()
+                for slot in range(HR * link, HR * (link + 1)):
+                    state[lax.rem(step, 2), ROWS + 2 * HS + slot] = land_reg[step, slot]
+
+    def take_sub_link(step, link, group):
+        @pl.when(has_target(1 - link, sub, last_sub))
+        def _():
+            sub_message(step, link, group).wait_recv()
+            for i in range(HS):
+                slot = HS * link + i
+                state[lax.rem(step, 2), ROWS + slot, part(group)] = land_sub[step, group, slot]
 
     def part(group):
         return slice(group * PART, (group + 1) * PART)
@@ -126,11 +131,9 @@
         for now in range(2):
             state[now, ROWS + slot] = zero
     probes_copy.wait()
-    for u in range(UNITS):
-        load_rows(u).start()
     for i in range(ROWS):
         state[0, i] = probes[:, i * BLK:(i + 1) * BLK]
-    peers = sum(jnp.where(sends, 1, 0) for _, _, _, _, sends, _ in links)
+    peers = sum(jnp.where(there, 1, 0) for _, _, there in peers_at)
     for slot, row in first_list + second_list:
         for group in range(GROUPS):
             out_sub[0, group, slot] = state[0, row, part(group)]
@@ -282,10 +285,10 @@
             for group in range(GROUPS):
                 take_sub_link(step, 1 - urgent, group)
                 multiply_group(now, taken, group, groups[group])
+                finish_urgent(group, groups[group])
+                send_sub_link(step + 1, urgent, group)
                 if group + 1 < GROUPS:
                     stage_others(rows)
-                finish_urgent(group, groups[group])
-                send_sub_link(step + 1, urgent, group)
             issue(now, [row for _, row in second_list], sets[1])
             issue(now, [row for _, row in third_list], sets[0])
             finish_second(sets[1])
@@ -335,11 +338,15 @@
     pl.run_scoped(run, *[pltpu.ACC(mxu_id=m)((height, 2 * BLK), F32) for height in heights for m in (0, 0, 1, 1)])
 
     def sent(step, carry):
-        for link in range(4):
-            for group in range(GROUPS if link < 2 else 1):
-                @pl.when(links[link][4])
-                def _():
-                    message(step, link, group).wait_send()
+        for link in range(2):
+            @pl.when(has_target(link, sub, last_sub))
+            def _():
+                for group in range(GROUPS):
+                    sub_message(step, link, group).wait_send()
+
+            @pl.when(has_target(link, region, last_region))
+            def _():
+                reg_message(step, link).wait_send()
         return carry
 
     lax.fori_loop(0, DEG, sent, 0)

time: 43.8 us -> 43.6 us (level)
  no operation moved by 1% of the time
where the time goes in v4:
time: 43.6 us
  Pallas kernels  42.4 us (97%)
  local copies, waits for them, and re-layouts  1.19 us (3%)
    pallas_call x1, Pallas kernels, local(): pl.pallas_call(kernel, out_shape=jax.ShapeDtypeStruct((PROBES, width), F3...  42.4 us
    unnamed x1, local copies, waits for them, and re-layouts  1.19 us

profile of v4, /device:TPU:6, one launch (start us, length us, event | category | flops | bytes accessed | tf_op | source)
XLA Modules:
  0.0 43.6 jit_solution(8208612968413751842)
XLA Ops:
  0.0 42.4 %shard_map.64 = f32[32,13312]{1,0:T(8,128)S(1)} custom-call(bf16[32,13312]{1,0:T(8,128)(2,1)} %probes_hbm.1, bf16[104,3,128,128]{3,2,1,0:T(8,128)(2,1)} %blocks_hbm.1, s32[3,104]{1,0:T(4,128)} %bitcast.1, s32[1,2,8]{2,1,0:T(2,128)} %sub_hbm.1, s32[1,2,4]{2,1,0:T(2,128)} %reg_hbm.1, f32[9]{0:T(128)} %coeffs_hbm.1), custom_call_target="tpu_custom_call" | custom-call | tf_op jit(solution)/shard_map/pallas_call | solution.py:359
  42.4 1.2 %copy.8 = f32[32,13312]{1,0:T(8,128)} copy(f32[32,13312]{1,0:T(8,128)S(1)} %shard_map.64) | data formatting | bytes 3407872

commit v5 on v4

--- a/solution.py
+++ b/solution.py
@@ -245,6 +245,18 @@
     def unit_rows(unit):
         return [unit * UNIT + i for i in range(UNIT)]
 
+    def sent(step, carry):
+        for link in range(2):
+            @pl.when(has_target(link, sub, last_sub))
+            def _():
+                for group in range(GROUPS):
+                    sub_message(step, link, group).wait_send()
+
+            @pl.when(has_target(link, region, last_region))
+            def _():
+                reg_message(step, link).wait_send()
+        return carry
+
     def run(*a):
         quads = [((a[i], a[i + 1]), (a[i + 2], a[i + 3])) for i in range(0, len(a), 4)]
         sets, groups = quads[:2], quads[2:]
@@ -302,7 +314,7 @@
                     finish_third(sets[0])
                     send_reg_links(step + 1)
             finish(UNITS - 1, sets[UNITS % 2])
-            return carry
+            return sent(step, carry)
 
         lax.fori_loop(0, DEG - 1, one_step, 0)
 
@@ -337,19 +349,7 @@
     heights = (2 * PROBES,) * 2 + (2 * PART,) * GROUPS
     pl.run_scoped(run, *[pltpu.ACC(mxu_id=m)((height, 2 * BLK), F32) for height in heights for m in (0, 0, 1, 1)])
 
-    def sent(step, carry):
-        for link in range(2):
-            @pl.when(has_target(link, sub, last_sub))
-            def _():
-                for group in range(GROUPS):
-                    sub_message(step, link, group).wait_send()
-
-            @pl.when(has_target(link, region, last_region))
-            def _():
-                reg_message(step, link).wait_send()
-        return carry
-
-    lax.fori_loop(0, DEG, sent, 0)
+    sent(DEG - 1, 0)
 
 
 def local(probes, blocks, col_slot, send_sub, send_reg, coeffs):

time: 43.6 us -> 43.5 us (level)
  no operation moved by 1% of the time
where the time goes in v5:
time: 43.5 us
  Pallas kernels  42.3 us (97%)
  local copies, waits for them, and re-layouts  1.19 us (3%)
    pallas_call x1, Pallas kernels, local(): pl.pallas_call(kernel, out_shape=jax.ShapeDtypeStruct((PROBES, width), F3...  42.3 us
    unnamed x1, local copies, waits for them, and re-layouts  1.19 us

profile of v5, /device:TPU:6, one launch (start us, length us, event | category | flops | bytes accessed | tf_op | source)
XLA Modules:
  0.0 43.5 jit_solution(4481710574844644668)
XLA Ops:
  0.0 42.3 %shard_map.64 = f32[32,13312]{1,0:T(8,128)S(1)} custom-call(bf16[32,13312]{1,0:T(8,128)(2,1)} %probes_hbm.1, bf16[104,3,128,128]{3,2,1,0:T(8,128)(2,1)} %blocks_hbm.1, s32[3,104]{1,0:T(4,128)} %bitcast.1, s32[1,2,8]{2,1,0:T(2,128)} %sub_hbm.1, s32[1,2,4]{2,1,0:T(2,128)} %reg_hbm.1, f32[9]{0:T(128)} %coeffs_hbm.1), custom_call_target="tpu_custom_call" | custom-call | tf_op jit(solution)/shard_map/pallas_call | solution.py:359
  42.3 1.2 %copy.8 = f32[32,13312]{1,0:T(8,128)} copy(f32[32,13312]{1,0:T(8,128)S(1)} %shard_map.64) | data formatting | bytes 3407872
